TPU v7x, 32 devices: a whole 2x2x4 slice. The times are simulated.
32 devices in a mesh: real: 2 (over y), rows: 4 (over z), orb: 4 (over x, core).
Axes of the slice: x: 2, y: 2, z: 4, core: 2. Of those that a mesh axis runs over, the one named last changes fastest.
Arguments:
- occupied: bfloat16 [2, 16, 256, 1024], P(None, ('real', 'rows'), None, 'orb'), parts along dimension 1, may hold values from -2.5 to 2.5
- disorder: int32 [16, 256], P(('real', 'rows')), parts along dimension 0, may hold values from -8 to 8
- region_cols: int32 [32], replicated, may hold values from 0 to 255, as said below
- cheb_coef: float32 [2, 8], replicated, may hold values from -0.6 to 0.6
- prior_corr: bfloat16 [2, 512, 256], P(None, ('real', 'rows'), 'orb'), parts along dimension 1, may hold values from -6 to 6
Outputs:
- correlation: float32 [2, 512, 256], P(None, ('real', 'rows'), 'orb'), parts along dimension 1
There are 2 independent parts, one for each index of `real`. A program takes and returns all parts, laid end to end along the dimension named above; an argument that names none is the same for every part. Nothing has to cross between parts.
Inputs may be any that keep to these rules, and one draw needn't show every extreme that they name: `region_cols`: 32 distinct columns; columns 0 and 255 are always among them.
All inputs are finite; a program needn't handle non-finite values.
Results may differ from a plain program's by a relative error of at most 0.0033.
Values may be sent and summed in bfloat16 or wider, within the bound.
A program may use at most 64 MiB of HBM per device.

v0:
```python
import functools

import jax
import jax.numpy as jnp
from jax import lax
from jax.experimental import pallas as pl
from jax.experimental.pallas import tpu as pltpu
from jax.sharding import PartitionSpec as P

HOP_SCALE = 5.25
LEVEL_STEP = 0.125


def padded_2(cells, sides, width):
    for axis, dim in sides:
        count = lax.axis_size(axis)
        head = lax.slice_in_dim(cells, 0, width, axis=dim)
        tail = lax.slice_in_dim(cells, cells.shape[dim] - width, cells.shape[dim], axis=dim)
        cells = jnp.concatenate(
            [
                lax.ppermute(tail, axis, [(i, (i + 1) % count) for i in range(count)]),
                cells,
                lax.ppermute(head, axis, [((i + 1) % count, i) for i in range(count)]),
            ],
            axis=dim,
        )
    return cells


def apply_rows(padded, onsite):
    middle = padded[:, 1:-1]
    neighbours = padded[:, 2:] + padded[:, :-2] + jnp.roll(middle, -1, 2) + jnp.roll(middle, 1, 2)
    return (onsite[None, :, :, None] * middle - neighbours) / HOP_SCALE


def rotate(picked):
    return jnp.stack([-picked[1], picked[0]])


def combine_pairs(products):
    return jnp.stack([products[0, 0] + products[1, 1], products[1, 0] - products[0, 1]])


def shards(occupied, disorder, region_cols, cheb_coef, prior_corr):
    band_rows = occupied.shape[1]
    term_count = cheb_coef.shape[1]
    current = occupied.astype(jnp.float32)

    def contribution(state, degree):
        picked = jnp.take(state, region_cols, axis=2)
        return cheb_coef[0, degree] * picked + cheb_coef[1, degree] * rotate(picked)

    summed = contribution(current, 0)
    previous = current
    onsite = disorder.astype(jnp.float32) * LEVEL_STEP
    for degree in range(1, term_count):
        padded = padded_2(current, (("rows", 1),), 1)
        applied = apply_rows(padded, onsite)
        following = applied if degree == 1 else 2.0 * applied - previous
        previous, current = (current, following)
        summed = summed + contribution(current, degree)
    tile_rows = band_rows * region_cols.shape[0]
    evolved = summed.astype(jnp.bfloat16).reshape(2, tile_rows, summed.shape[3])
    row_panel = lax.all_gather(evolved, "orb", axis=2, tiled=True)
    column_all = lax.all_gather(evolved, "rows", axis=1, tiled=True)
    column_panel = lax.all_to_all(column_all, "orb", split_axis=1, concat_axis=2, tiled=True)
    products = jnp.einsum(
        "cim,djm->cdij", row_panel, column_panel, preferred_element_type=jnp.float32
    )
    tile_sum = combine_pairs(products)
    return prior_corr.astype(jnp.float32) + tile_sum


LANES = 128
MESH = pl.DeviceIdType.MESH


def quench_kernel(
    row_count, occupied, disorder, region_cols, cheb_coef, prior, out,
    fields, levels, hot, window, operator, product, shares, rounded, base, crossed,
    evolved, partial, outgoing, incoming,
    level_send, level_recv, field_send, field_recv, base_send, base_recv,
    cross_send, cross_recv, half_send, half_recv, block_send, block_recv,
):
    r = lax.axis_index("rows")
    o = lax.axis_index("orb")
    g = o % 2
    x = o // 2
    mate = 2 * x + 1 - g
    band, width = disorder.shape
    height = band * row_count
    terms = cheb_coef.shape[1]
    reach = terms - 1
    acols = region_cols.shape[0]
    tile = prior.shape[1]
    chips = 2 * row_count
    mine = 2 * r + x
    half = row_count // 2
    side = r // half
    place = r % half
    pair = r + 1 - 2 * place
    across = (r + half) % row_count
    owner = g == side

    def remote(src, dst, send, recv, row, orb):
        return pltpu.make_async_remote_copy(
            src_ref=src, dst_ref=dst, send_sem=send, recv_sem=recv,
            device_id={"rows": row, "orb": orb}, device_id_type=MESH,
        )

    row_id = lax.broadcasted_iota(jnp.int32, (height, width), 0)
    own = disorder[...].astype(jnp.float32) * LEVEL_STEP
    slab = jnp.zeros((height, width), jnp.float32)
    for i in range(band):
        slab = jnp.where(row_id == band * r + i, own[i : i + 1, :], slab)
    levels[r] = slab

    barrier = pltpu.get_barrier_semaphore()

    def greet(row, orb):
        pl.semaphore_signal(
            barrier, inc=1, device_id={"rows": row, "orb": orb}, device_id_type=MESH
        )

    has_left, has_right = r > 0, r < row_count - 1
    greet(r, mate)
    greet(r, (o + 2) % 4)
    pl.when(has_left)(lambda: greet((r + row_count - 1) % row_count, o))
    pl.when(has_right)(lambda: greet((r + 1) % row_count, o))
    pl.semaphore_wait(
        barrier, 2 + jnp.where(has_left, 1, 0) + jnp.where(has_right, 1, 0)
    )

    def level_copy(slot, way):
        return remote(
            levels.at[slot], levels.at[slot], level_send.at[(way + 1) // 2, slot],
            level_recv.at[slot], (r + row_count + way) % row_count, o,
        )

    pl.when(has_left)(lambda: level_copy(r, -1).start())
    pl.when(has_right)(lambda: level_copy(r, 1).start())

    def chunk(i, which):
        return occupied.at[:, i, :, pl.ds(pl.multiple_of(which * LANES, LANES), LANES)]

    def field_copy(i):
        return remote(
            chunk(i, 1 - place), fields.at[place, i], field_send.at[i],
            field_recv.at[place, i], pair, o,
        )

    for i in range(band):
        field_copy(i).start()
    for i in range(band):
        pltpu.make_async_copy(
            chunk(i, place), fields.at[place, i], field_recv.at[place, i]
        ).start()

    lane = lax.broadcasted_iota(jnp.int32, (1, LANES), 1)
    cols = jnp.zeros((1, LANES), jnp.int32)
    for a in range(acols):
        cols = jnp.where(lane % acols == a, region_cols[a], cols)
    offset = lax.broadcasted_iota(jnp.int32, (width, LANES), 0) - cols + reach
    offset = jnp.where(offset < 0, offset + width, offset)
    offset = jnp.where(offset >= width, offset - width, offset)

    for d in range(1, 2 * reach):
        hot[d - 1] = jnp.where(offset == d, 1.0, 0.0).astype(jnp.bfloat16)

    for hop in range(1, row_count):
        for way in (1, -1):
            slot = (r + row_count - way * hop) % row_count
            follows = r + way
            here = r >= hop if way == 1 else r + hop < row_count

            @pl.when(here)
            def _():
                remote(
                    levels.at[slot], levels.at[slot], level_send.at[0, slot],
                    level_recv.at[slot], (r + row_count - way) % row_count, o,
                ).wait_recv()

                @pl.when((follows >= 0) & (follows < row_count))
                def _():
                    level_copy(slot, way).start()

    onsite = levels[0]
    for slot in range(1, row_count):
        onsite = onsite + levels[slot]
    onsite = onsite.astype(jnp.bfloat16)

    local_levels = {}
    for d in range(1, 2 * reach):
        here = jnp.dot(onsite, hot[d - 1], preferred_element_type=jnp.float32)
        local_levels[d] = jnp.concatenate([here, here], axis=1)

    lane = lax.broadcasted_iota(jnp.int32, (height, 2 * LANES), 1)
    row_id = lax.broadcasted_iota(jnp.int32, (height, 2 * LANES), 0)
    start = jnp.where(row_id == lane // acols, 1.0, 0.0)
    previous, current = {}, {reach: start}
    real = {reach: cheb_coef[0, 0] * start}
    imag = {reach: cheb_coef[1, 0] * start}
    for degree in range(1, terms):
        following = {}
        for d in range(reach - degree, reach + degree + 1):
            total = None
            if d in current:
                here = current[d]
                total = local_levels[d] * here - (
                    pltpu.roll(here, 1, 0) + pltpu.roll(here, height - 1, 0)
                )
            for beside in (d - 1, d + 1):
                if beside in current:
                    there = current[beside]
                    total = -there if total is None else total - there
            value = total * ((1.0 if degree == 1 else 2.0) / HOP_SCALE)
            if d in previous:
                value = value - previous[d]
            following[d] = value
            more_real = cheb_coef[0, degree] * value
            more_imag = cheb_coef[1, degree] * value
            real[d] = real[d] + more_real if d in real else more_real
            imag[d] = imag[d] + more_imag if d in imag else more_imag
        previous, current = current, following
    for d in range(2 * reach + 1):
        for part, parts in ((0, real), (1, imag)):
            for group in range(2):
                window[part, group, d] = parts[d][:, group * LANES : (group + 1) * LANES]

    depth = height // 2

    def expand(y, carry):
        for part in range(2):
            for group in range(2):
                dense = jnp.zeros((width, LANES), jnp.float32)
                for d in range(2 * reach + 1):
                    value = window[part, group, d, pl.ds(depth * side + y, 1), :]
                    dense = jnp.where(offset == d, value, dense)
                dense = dense.T
                high = dense.astype(jnp.bfloat16)
                low = (dense - high.astype(jnp.float32)).astype(jnp.bfloat16)
                sites = pl.ds((2 * part + group) * LANES, LANES)
                operator[0, y, sites, :] = high
                operator[1, y, sites, :] = low
        return carry

    lax.fori_loop(0, depth, expand, 0)

    for step in range(half):
        slot = (place + step) % half
        for i in range(band):
            remote(
                fields.at[slot, i], fields.at[slot, i], field_send.at[i],
                field_recv.at[slot, i], pair, o,
            ).wait_recv()
            both = jnp.concatenate([fields[slot, i, 0], fields[slot, i, 1]], axis=1)
            row = band * slot + i
            more = jnp.dot(
                operator[0, row], both, preferred_element_type=jnp.float32
            ) + jnp.dot(operator[1, row], both, preferred_element_type=jnp.float32)
            if step or i:
                more = product[...] + more
            product[...] = more
    for s in range(2):
        top = pl.ds(s * LANES, LANES)
        low = pl.ds((2 + s) * LANES, LANES)
        first, second = pl.ds(0, LANES), pl.ds(LANES, LANES)
        share0 = product[top, first] - product[low, second]
        share1 = product[top, second] + product[low, first]
        shares[s, 0] = share0
        shares[s, 1] = share1
        rounded[s, 0] = share0.astype(jnp.bfloat16)
        rounded[s, 1] = share1.astype(jnp.bfloat16)

    def base_copy():
        return remote(shares.at[1 - g], base, base_send, base_recv, r, mate)

    def cross_copy(s):
        return remote(
            rounded.at[s], crossed, cross_send.at[s], cross_recv, across, 2 * x + s
        )

    @pl.when(owner)
    def _():
        base_copy().start()
        pltpu.make_async_copy(shares.at[g], base, base_recv).start()

    @pl.when(jnp.logical_not(owner))
    def _():
        for s in range(2):
            cross_copy(s).start()

    base_copy().wait_recv()
    cross_copy(0).wait_recv()
    evolved[g] = (base[...] + crossed[...].astype(jnp.float32)).astype(jnp.bfloat16)

    def half_copy(slot):
        return remote(
            evolved.at[slot], evolved.at[slot], half_send, half_recv, r, mate
        )

    half_copy(g).start()
    half_copy(1 - g).wait_recv()

    left = jnp.concatenate(
        [jnp.concatenate([evolved[s, 0], evolved[s, 1]], axis=1) for s in range(2)], axis=0
    )
    columns = pl.ds(pl.multiple_of(g * tile, tile), tile)
    rights = []
    for s in range(2):
        p0 = evolved[s, 0, columns, :]
        p1 = evolved[s, 1, columns, :]
        rights.append(jnp.concatenate([p0, p1], axis=1))
        rights.append(jnp.concatenate([-p1, p0], axis=1))
    right = jnp.concatenate(rights, axis=0)
    blocks = lax.dot_general(
        left, right, (((1,), (1,)), ((), ())), preferred_element_type=jnp.float32
    )
    for s in range(2):
        for row in range(row_count):
            block = blocks[row * tile : (row + 1) * tile, s * LANES : (s + 1) * LANES]
            partial[2 * row + s] = block
            outgoing[2 * row + s] = block.astype(jnp.bfloat16)

    def block_copy(k, slot):
        to = (mine + k) % chips
        return remote(
            outgoing.at[to], incoming.at[slot], block_send.at[k - 1],
            block_recv.at[slot], to // 2, 2 * (to % 2) + g,
        )

    for k in range(1, chips):
        block_copy(k, mine).start()
    total = partial[mine]
    for k in range(1, chips):
        slot = (mine + chips - k) % chips
        block_copy(k, slot).wait_recv()
        total = total + incoming[slot].astype(jnp.float32)
    out[0] = prior[0].astype(jnp.float32) + total[:, :tile]
    out[1] = prior[1].astype(jnp.float32) + total[:, tile:]

    for hop in range(row_count):
        for way in (1, -1):
            slot = (r + row_count - way * hop) % row_count
            follows = r + way
            here = r >= hop if way == 1 else r + hop < row_count

            @pl.when(here & (follows >= 0) & (follows < row_count))
            def _():
                level_copy(slot, way).wait_send()

    for i in range(band):
        field_copy(i).wait_send()
    pl.when(owner)(lambda: base_copy().wait_send())

    @pl.when(jnp.logical_not(owner))
    def _():
        for s in range(2):
            cross_copy(s).wait_send()

    half_copy(g).wait_send()
    for k in range(1, chips):
        block_copy(k, mine).wait_send()


def fused_step(row_count, occupied, disorder, region_cols, cheb_coef, prior_corr):
    band, width = disorder.shape
    terms = cheb_coef.shape[1]
    tile = prior_corr.shape[1]
    height = band * row_count
    chips = 2 * row_count
    half = row_count // 2
    dma = pltpu.SemaphoreType.DMA
    vmem = pl.BlockSpec(memory_space=pltpu.VMEM)
    smem = pl.BlockSpec(memory_space=pltpu.SMEM)
    return pl.pallas_call(
        functools.partial(quench_kernel, row_count),
        out_shape=jax.ShapeDtypeStruct(prior_corr.shape, jnp.float32),
        in_specs=[pl.BlockSpec(memory_space=pl.ANY), vmem, smem, smem, vmem],
        out_specs=vmem,
        scratch_shapes=[
            pltpu.VMEM((half, band, 2, width, LANES), jnp.bfloat16),
            pltpu.VMEM((row_count, height, width), jnp.float32),
            pltpu.VMEM((2 * terms - 3, width, LANES), jnp.bfloat16),
            pltpu.VMEM((2, 2, 2 * terms - 1, height, LANES), jnp.float32),
            pltpu.VMEM((2, height // 2, 4 * LANES, width), jnp.bfloat16),
            pltpu.VMEM((4 * LANES, 2 * LANES), jnp.float32),
            pltpu.VMEM((2, 2, LANES, LANES), jnp.float32),
            pltpu.VMEM((2, 2, LANES, LANES), jnp.bfloat16),
            pltpu.VMEM((2, LANES, LANES), jnp.float32),
            pltpu.VMEM((2, LANES, LANES), jnp.bfloat16),
            pltpu.VMEM((2, 2, LANES, LANES), jnp.bfloat16),
            pltpu.VMEM((chips, tile, LANES), jnp.float32),
            pltpu.VMEM((chips, tile, LANES), jnp.bfloat16),
            pltpu.VMEM((chips, tile, LANES), jnp.bfloat16),
            dma((2, row_count)),
            dma((row_count,)),
            dma((band,)),
            dma((half, band)),
            dma,
            dma,
            dma((2,)),
            dma,
            dma,
            dma,
            dma((chips - 1,)),
            dma((chips,)),
        ],
        compiler_params=pltpu.CompilerParams(collective_id=0, has_side_effects=True),
    )(occupied, disorder, region_cols, cheb_coef, prior_corr)


def local_step(row_count, orb_count, occupied, disorder, region_cols, cheb_coef, prior_corr):
    band, width, orbitals = occupied.shape[1:]
    terms = cheb_coef.shape[1]
    height = band * row_count
    sites = height * region_cols.shape[0]
    fused = (
        orb_count == 4
        and sites == 2 * LANES
        and 2 * orbitals == row_count * LANES
        and orbitals == 2 * LANES
        and height % 8 == 0
        and width % LANES == 0
        and width >= 2 * terms
        and LANES % region_cols.shape[0] == 0
        and prior_corr.shape[1:] == (LANES // 2, LANES // 2)
    )
    if fused:
        return fused_step(row_count, occupied, disorder, region_cols, cheb_coef, prior_corr)
    return shards(occupied, disorder, region_cols, cheb_coef, prior_corr)


def solution(mesh):
    return jax.shard_map(
        functools.partial(local_step, mesh.shape["rows"], mesh.shape["orb"]),
        mesh=mesh,
        in_specs=(
            P(None, ("real", "rows"), None, "orb"),
            P(("real", "rows"), None),
            P(),
            P(),
            P(None, ("real", "rows"), "orb"),
        ),
        out_specs=P(None, ("real", "rows"), "orb"),
        check_vma=False,
    )
```

profile of v0, /device:TPU:0, one launch (start us, length us, event | category | flops | bytes accessed | tf_op | source)
XLA Modules:
  0.0 29.0 jit_solution(2884581838293346633)
XLA Ops:
  0.0 27.5 %shard_map.55 = f32[2,64,64]{2,1,0:T(8,128)} custom-call(bf16[2,2,256,256]{3,2,1,0:T(8,128)(2,1)} %occupied.1, s32[2,256]{1,0:T(2,128)} %disorder.1, s32[32]{0:T(128)} %region_cols.1, f32[2,8]{1,0:T(2,128)} %cheb_coef.1, bf16[2,64,64]{2,1,0:T(8,128)(2,1)} %prior.1), custom_call_target="tpu_custom_call" | custom-call | tf_op jit(solution)/shard_map/pallas_call | solution.py:376
  27.5 1.5 %copy.7 = f32[2,64,64]{2,1,0:T(8,128)} copy(f32[2,64,64]{2,1,0:T(8,128)} %shard_map.55) | data formatting | bytes 65536
where the time goes:
time: 29.2 us; the launch traced here: 29 us
  Pallas kernels  27.5 us (94%)
  local copies, waits for them, and re-layouts  1.47 us (5%)
    pallas_call x1, Pallas kernels, fused_step(): pl.pallas_call(functools.partial(quench_kernel, row_count), out_shape=jax...  27.5 us
    unnamed x1, local copies, waits for them, and re-layouts  1.47 us

commit v1 on v0

v1 whole, which is shorter than its diff:
```python
import functools

import jax
import jax.numpy as jnp
from jax import lax
from jax.experimental import pallas as pl
from jax.experimental.pallas import tpu as pltpu
from jax.sharding import PartitionSpec as P

HOP_SCALE = 5.25
LEVEL_STEP = 0.125


def padded_2(cells, sides, width):
    for axis, dim in sides:
        count = lax.axis_size(axis)
        head = lax.slice_in_dim(cells, 0, width, axis=dim)
        tail = lax.slice_in_dim(cells, cells.shape[dim] - width, cells.shape[dim], axis=dim)
        cells = jnp.concatenate(
            [
                lax.ppermute(tail, axis, [(i, (i + 1) % count) for i in range(count)]),
                cells,
                lax.ppermute(head, axis, [((i + 1) % count, i) for i in range(count)]),
            ],
            axis=dim,
        )
    return cells


def apply_rows(padded, onsite):
    middle = padded[:, 1:-1]
    neighbours = padded[:, 2:] + padded[:, :-2] + jnp.roll(middle, -1, 2) + jnp.roll(middle, 1, 2)
    return (onsite[None, :, :, None] * middle - neighbours) / HOP_SCALE


def rotate(picked):
    return jnp.stack([-picked[1], picked[0]])


def combine_pairs(products):
    return jnp.stack([products[0, 0] + products[1, 1], products[1, 0] - products[0, 1]])


def shards(occupied, disorder, region_cols, cheb_coef, prior_corr):
    band_rows = occupied.shape[1]
    term_count = cheb_coef.shape[1]
    current = occupied.astype(jnp.float32)

    def contribution(state, degree):
        picked = jnp.take(state, region_cols, axis=2)
        return cheb_coef[0, degree] * picked + cheb_coef[1, degree] * rotate(picked)

    summed = contribution(current, 0)
    previous = current
    onsite = disorder.astype(jnp.float32) * LEVEL_STEP
    for degree in range(1, term_count):
        padded = padded_2(current, (("rows", 1),), 1)
        applied = apply_rows(padded, onsite)
        following = applied if degree == 1 else 2.0 * applied - previous
        previous, current = (current, following)
        summed = summed + contribution(current, degree)
    tile_rows = band_rows * region_cols.shape[0]
    evolved = summed.astype(jnp.bfloat16).reshape(2, tile_rows, summed.shape[3])
    row_panel = lax.all_gather(evolved, "orb", axis=2, tiled=True)
    column_all = lax.all_gather(evolved, "rows", axis=1, tiled=True)
    column_panel = lax.all_to_all(column_all, "orb", split_axis=1, concat_axis=2, tiled=True)
    products = jnp.einsum(
        "cim,djm->cdij", row_panel, column_panel, preferred_element_type=jnp.float32
    )
    tile_sum = combine_pairs(products)
    return prior_corr.astype(jnp.float32) + tile_sum


LANES = 128
FRAME = 16
MESH = pl.DeviceIdType.MESH


def quench_kernel(
    row_count, occupied, disorder, region_cols, cheb_coef, out,
    fields, turned, levels, hot, window, picks, operator, product, kept, leaving,
    crossed, outgoing, incoming, columns, weights,
    load_sem, level_send, level_recv, field_send, field_recv,
    cross_send, cross_recv, block_send, block_recv,
):
    r = lax.axis_index("rows")
    o = lax.axis_index("orb")
    g = o % 2
    x = o // 2
    band, width = disorder.shape
    height = band * row_count
    terms = cheb_coef.shape[1]
    reach = terms - 1
    acols = region_cols.shape[0]
    tile = out.shape[1]
    chips = 2 * row_count
    mine = 2 * r + x
    half = row_count // 2
    side = r // half
    place = r % half
    pair = r + 1 - 2 * place
    across = (r + half) % row_count
    owner = g == side
    spots = 2 * LANES

    def remote(src, dst, send, recv, row, orb):
        return pltpu.make_async_remote_copy(
            src_ref=src, dst_ref=dst, send_sem=send, recv_sem=recv,
            device_id={"rows": row, "orb": orb}, device_id_type=MESH,
        )

    barrier = pltpu.get_barrier_semaphore()

    def greet(row, orb):
        pl.semaphore_signal(
            barrier, inc=1, device_id={"rows": row, "orb": orb}, device_id_type=MESH
        )

    has_left, has_right = r > 0, r < row_count - 1
    pl.when(has_left)(lambda: greet((r + row_count - 1) % row_count, o))
    pl.when(has_right)(lambda: greet((r + 1) % row_count, o))
    for k in range(1, 4):
        greet(r, (o + k) % 4)

    def chunk(i, which):
        return occupied.at[:, i, :, pl.ds(pl.multiple_of(which * LANES, LANES), LANES)]

    loads = [
        pltpu.make_async_copy(disorder, levels.at[r], load_sem.at[0]),
        pltpu.make_async_copy(region_cols, columns, load_sem.at[1]),
        pltpu.make_async_copy(cheb_coef, weights, load_sem.at[2]),
    ]
    for load in loads:
        load.start()
    own_loads = [
        pltpu.make_async_copy(chunk(i, place), fields.at[0, i], field_recv.at[0, i])
        for i in range(band)
    ]
    for load in own_loads:
        load.start()
    for load in loads:
        load.wait()

    pl.semaphore_wait(
        barrier, 3 + jnp.where(has_left, 1, 0) + jnp.where(has_right, 1, 0)
    )

    def level_copy(first, count, way, kind, row):
        part = levels.at[pl.ds(first, count)]
        return remote(part, part, level_send.at[kind], level_recv.at[way], row, o)

    to_left = functools.partial(level_copy, r, 1, 1, 0, (r + row_count - 1) % row_count)
    to_right = functools.partial(level_copy, r, 1, 0, 1, (r + 1) % row_count)
    pl.when(has_left)(lambda: to_left().start())
    pl.when(has_right)(lambda: to_right().start())

    def field_copy(i):
        return remote(
            chunk(i, 1 - place), fields.at[1, i], field_send.at[i],
            field_recv.at[1, i], pair, o,
        )

    for i in range(band):
        field_copy(i).start()

    lane = lax.broadcasted_iota(jnp.int32, (1, LANES), 1)
    cols = jnp.zeros((1, LANES), jnp.int32)
    for a in range(acols):
        cols = jnp.where(lane % acols == a, columns[a], cols)
    offset = lax.broadcasted_iota(jnp.int32, (width, LANES), 0) - cols + reach
    offset = jnp.where(offset < 0, offset + width, offset)
    offset = jnp.where(offset >= width, offset - width, offset)
    for d in range(1, 2 * reach):
        hot[d - 1] = jnp.where(offset == d, 1.0, 0.0).astype(jnp.bfloat16)

    first = cols - reach
    first = jnp.where(first < 0, first + width, first)
    first = jnp.concatenate([first, first], axis=1)
    slide = jnp.broadcast_to(first % FRAME, (2 * FRAME, spots))
    strip = jnp.broadcast_to(first // FRAME, (FRAME, spots))
    strips = width // FRAME
    for j in range(strips):
        picks[j] = jnp.where(strip == j, 1.0, 0.0).astype(jnp.bfloat16)

    def turn(slot, i):
        k = band * slot + i
        for part in range(2):
            turned[part * LANES : (part + 1) * LANES, k * width : (k + 1) * width] = (
                fields[slot, i, part].T
            )

    for i in range(band):
        own_loads[i].wait()
        turn(0, i)

    @pl.when(has_left)
    def _():
        level_copy((r + row_count - 1) % row_count, 1, 0, 1, r).wait_recv()

    @pl.when(has_right)
    def _():
        level_copy((r + 1) % row_count, 1, 1, 0, r).wait_recv()

    middle = (r > 0) & (r < row_count - 1)
    behind = (row_count - 1) * side
    both_far = functools.partial(level_copy, half * side, half, 2, 2, (row_count - 1) * (1 - side))
    one_near = functools.partial(level_copy, behind, 1, 2, 3, row_count - 1 - r)

    @pl.when(middle)
    def _():
        both_far().start()
        one_near().start()
        level_copy((row_count - 1) * (1 - side), 1, 2, 3, r).wait_recv()

    @pl.when(jnp.logical_not(middle))
    def _():
        level_copy(half * (1 - side), half, 2, 2, r).wait_recv()

    onsite = jnp.concatenate([levels[k] for k in range(row_count)], axis=0)
    onsite = (onsite.astype(jnp.float32) * LEVEL_STEP).astype(jnp.bfloat16)

    local_levels = {}
    for d in range(1, 2 * reach):
        here = jnp.dot(onsite, hot[d - 1], preferred_element_type=jnp.float32)
        local_levels[d] = jnp.concatenate([here, here], axis=1)

    lane = lax.broadcasted_iota(jnp.int32, (height, spots), 1)
    row_id = lax.broadcasted_iota(jnp.int32, (height, spots), 0)
    start = jnp.where(row_id == lane // acols, 1.0, 0.0)
    previous, current = {}, {reach: start}
    real = {reach: weights[0, 0] * start}
    imag = {reach: weights[1, 0] * start}
    for degree in range(1, terms):
        following = {}
        for d in range(reach - degree, reach + degree + 1):
            total = None
            if d in current:
                here = current[d]
                total = local_levels[d] * here - (
                    pltpu.roll(here, 1, 0) + pltpu.roll(here, height - 1, 0)
                )
            for beside in (d - 1, d + 1):
                if beside in current:
                    there = current[beside]
                    total = -there if total is None else total - there
            value = total * ((1.0 if degree == 1 else 2.0) / HOP_SCALE)
            if d in previous:
                value = value - previous[d]
            following[d] = value
            more_real = weights[0, degree] * value
            more_imag = weights[1, degree] * value
            real[d] = real[d] + more_real if d in real else more_real
            imag[d] = imag[d] + more_imag if d in imag else more_imag
        previous, current = current, following
    for part, parts in ((0, real), (1, imag)):
        for d in range(FRAME):
            rows = pl.ds((part * FRAME + d) * height, height)
            value = parts[d] if d in parts else jnp.zeros((height, spots), jnp.float32)
            window[0, rows, :] = value[:, :LANES]
            window[1, rows, :] = value[:, LANES:]

    def expand(slot, i):
        k = band * slot + i
        where = place if slot == 0 else 1 - place
        y = band * (half * side + where) + i
        for part in range(2):
            rows = pl.ds(part * FRAME * height + y, FRAME, stride=height)
            bare = jnp.concatenate([window[0, rows, :], window[1, rows, :]], axis=1)
            frame = jnp.concatenate([bare, jnp.zeros_like(bare)], axis=0)
            step = 1
            while step < FRAME:
                moved = pltpu.roll(frame, step, 0)
                frame = jnp.where((slide & step) != 0, moved, frame)
                step *= 2
            high = frame.astype(jnp.bfloat16)
            low = (frame - high.astype(jnp.float32)).astype(jnp.bfloat16)
            for kind, value in ((0, high), (1, low)):
                upper, lower = value[:FRAME], value[FRAME:]
                for j in range(strips):
                    operator[
                        kind, k * width + j * FRAME : k * width + (j + 1) * FRAME,
                        part * spots : (part + 1) * spots,
                    ] = upper * picks[j] + lower * picks[(j - 1) % strips]

    def applied(slot):
        rows = slice(slot * band * width, (slot + 1) * band * width)
        return jnp.dot(
            turned[:, rows], operator[0, rows, :], preferred_element_type=jnp.float32
        ) + jnp.dot(turned[:, rows], operator[1, rows, :], preferred_element_type=jnp.float32)

    for i in range(band):
        expand(0, i)
    product[...] = applied(0)
    for i in range(band):
        expand(1, i)
    for i in range(band):
        remote(
            fields.at[1, i], fields.at[1, i], field_send.at[i], field_recv.at[1, i], pair, o
        ).wait_recv()
        turn(1, i)
    total = product[...] + applied(1)
    sum0 = total[:LANES, :spots] - total[LANES:, spots:]
    sum1 = total[LANES:, :spots] + total[:LANES, spots:]

    def cross_copy():
        return remote(leaving, crossed, cross_send, cross_recv, across, o)

    def block_copy(k, part, slot):
        to = (mine + k) % chips
        place_of = 2 * to + part
        return remote(
            outgoing.at[place_of], incoming.at[slot], block_send.at[2 * k + part],
            block_recv.at[slot], to // 2, 2 * (to % 2) + part,
        )

    def mate_copy():
        return remote(
            outgoing.at[2 * mine + 1 - g], incoming.at[mine], block_send.at[0],
            block_recv.at[mine], r, 2 * x + 1 - g,
        )

    @pl.when(jnp.logical_not(owner))
    def _():
        leaving[0] = sum0.astype(jnp.bfloat16)
        leaving[1] = sum1.astype(jnp.bfloat16)
        cross_copy().start()

    @pl.when(owner)
    def _():
        kept[0] = sum0
        kept[1] = sum1
        cross_copy().wait_recv()
        evolved = [
            (kept[part] + crossed[part].astype(jnp.float32)).astype(jnp.bfloat16).T
            for part in range(2)
        ]
        left = jnp.concatenate([evolved[0], evolved[1]], axis=1)
        flipped = jnp.concatenate([-evolved[1], evolved[0]], axis=1)
        rights = []
        for column in range(4):
            rows = slice(column * tile, (column + 1) * tile)
            rights.append(left[rows])
            rights.append(flipped[rows])
        blocks = lax.dot_general(
            left, jnp.concatenate(rights, axis=0), (((1,), (1,)), ((), ())),
            preferred_element_type=jnp.float32,
        ).astype(jnp.bfloat16)
        for row in range(row_count):
            for column in range(4):
                outgoing[4 * row + column] = blocks[
                    row * tile : (row + 1) * tile, column * LANES : (column + 1) * LANES
                ]
        for k in range(chips - 1, 0, -1):
            for part in range(2):
                block_copy(k, part, mine).start()
        mate_copy().start()
        incoming[mine] = outgoing[2 * mine + g]

    pl.when(jnp.logical_not(owner))(lambda: mate_copy().wait_recv())
    total = incoming[mine].astype(jnp.float32)
    for k in range(1, chips):
        slot = (mine + chips - k) % chips
        block_copy(k, 0, slot).wait_recv()
        total = total + incoming[slot].astype(jnp.float32)
    out[0] = total[:, :tile]
    out[1] = total[:, tile:]

    pl.when(has_left)(lambda: to_left().wait_send())
    pl.when(has_right)(lambda: to_right().wait_send())

    @pl.when(middle)
    def _():
        both_far().wait_send()
        one_near().wait_send()

    for i in range(band):
        field_copy(i).wait_send()
    pl.when(jnp.logical_not(owner))(lambda: cross_copy().wait_send())

    @pl.when(owner)
    def _():
        mate_copy().wait_send()
        for k in range(1, chips):
            for part in range(2):
                block_copy(k, part, mine).wait_send()


def fused_step(row_count, occupied, disorder, region_cols, cheb_coef, prior_corr):
    band, width = disorder.shape
    terms = cheb_coef.shape[1]
    tile = prior_corr.shape[1]
    height = band * row_count
    chips = 2 * row_count
    half = row_count // 2
    spots = 2 * LANES
    dma = pltpu.SemaphoreType.DMA
    anywhere = pl.BlockSpec(memory_space=pl.ANY)
    corr = pl.pallas_call(
        functools.partial(quench_kernel, row_count),
        out_shape=pltpu.VMEM(prior_corr.shape, jnp.float32),
        in_specs=[anywhere] * 4,
        out_specs=pl.BlockSpec(memory_space=pltpu.VMEM),
        scratch_shapes=[
            pltpu.VMEM((2, band, 2, width, LANES), jnp.bfloat16),
            pltpu.VMEM((2 * LANES, height // 2 * width), jnp.bfloat16),
            pltpu.VMEM((row_count, band, width), jnp.int32),
            pltpu.VMEM((2 * terms - 3, width, LANES), jnp.bfloat16),
            pltpu.VMEM((2, 2 * FRAME * height, LANES), jnp.float32),
            pltpu.VMEM((width // FRAME, FRAME, spots), jnp.bfloat16),
            pltpu.VMEM((2, height // 2 * width, 2 * spots), jnp.bfloat16),
            pltpu.VMEM((2 * LANES, 2 * spots), jnp.float32),
            pltpu.VMEM((2, LANES, spots), jnp.float32),
            pltpu.VMEM((2, LANES, spots), jnp.bfloat16),
            pltpu.VMEM((2, LANES, spots), jnp.bfloat16),
            pltpu.VMEM((2 * chips, tile, LANES), jnp.bfloat16),
            pltpu.VMEM((chips, tile, LANES), jnp.bfloat16),
            pltpu.SMEM(region_cols.shape, jnp.int32),
            pltpu.SMEM(cheb_coef.shape, jnp.float32),
            dma((3,)),
            dma((4,)),
            dma((3,)),
            dma((band,)),
            dma((2, band)),
            dma,
            dma,
            dma((2 * chips,)),
            dma((chips,)),
        ],
        compiler_params=pltpu.CompilerParams(collective_id=0, has_side_effects=True),
    )(occupied, disorder, region_cols, cheb_coef)
    return prior_corr.astype(jnp.float32) + corr


def local_step(row_count, orb_count, occupied, disorder, region_cols, cheb_coef, prior_corr):
    band, width, orbitals = occupied.shape[1:]
    terms = cheb_coef.shape[1]
    height = band * row_count
    sites = height * region_cols.shape[0]
    fused = (
        orb_count == 4
        and row_count == 4
        and sites == 2 * LANES
        and 2 * orbitals == row_count * LANES
        and orbitals == 2 * LANES
        and height % 8 == 0
        and width % LANES == 0
        and width >= 2 * FRAME
        and 2 * terms <= FRAME
        and LANES % region_cols.shape[0] == 0
        and prior_corr.shape[1:] == (LANES // 2, LANES // 2)
    )
    if fused:
        return fused_step(row_count, occupied, disorder, region_cols, cheb_coef, prior_corr)
    return shards(occupied, disorder, region_cols, cheb_coef, prior_corr)


def solution(mesh):
    return jax.shard_map(
        functools.partial(local_step, mesh.shape["rows"], mesh.shape["orb"]),
        mesh=mesh,
        in_specs=(
            P(None, ("real", "rows"), None, "orb"),
            P(("real", "rows"), None),
            P(),
            P(),
            P(None, ("real", "rows"), "orb"),
        ),
        out_specs=P(None, ("real", "rows"), "orb"),
        check_vma=False,
    )
```

time: 29.2 us -> 26.2 us (0.90)
  Pallas kernels: 27.5 us -> 25.4 us
  local copies, waits for them, and re-layouts: 1.47 us -> 0.01 us
  other arithmetic: 0 us -> 0.64 us
    pallas_call x1, Pallas kernels: 27.5 us -> 25.4 us  [fused_step(): pl.pallas_call(functools.partial(quench_kernel, row_count), out_shape=plt...]
    unnamed x1 -> x2, local copies, waits for them, and re-layouts: 1.47 us -> 0.01 us
    add x0 -> x1, other arithmetic: none -> 0.64 us  [fused_step(): return prior_corr.astype(jnp.float32) + corr]
where the time goes in v1:
time: 26.2 us; the launch traced here: 26.1 us
  Pallas kernels  25.4 us (97%)
  other arithmetic  0.64 us (2%)
    pallas_call x1, Pallas kernels, fused_step(): pl.pallas_call(functools.partial(quench_kernel, row_count), out_shape=plt...  25.4 us
    add x1, other arithmetic, fused_step(): return prior_corr.astype(jnp.float32) + corr  0.64 us

profile of v1, /device:TPU:0, one launch (start us, length us, event | category | flops | bytes accessed | tf_op | source)
XLA Modules:
  0.0 26.1 jit_solution(4924585189145565011)
XLA Ops:
  0.0 0.0 copy-start
  0.0 25.4 %shard_map.55 = f32[2,64,64]{2,1,0:T(8,128)S(1)} custom-call(bf16[2,2,256,256]{3,2,1,0:T(8,128)(2,1)} %occupied.1, s32[2,256]{1,0:T(2,128)} %disorder.1, s32[32]{0:T(128)} %region_cols.1, f32[2,8]{1,0:T(2,128)} %cheb_coef.1), custom_call_target="tpu_custom_call" | custom-call | tf_op jit(solution)/shard_map/pallas_call | solution.py:398
  25.4 0.0 copy-done
  25.4 0.6 %convert_add_fusion = f32[2,64,64]{2,1,0:T(8,128)} fusion(f32[2,64,64]{2,1,0:T(8,128)S(1)} %shard_map.55, bf16[2,64,64]{2,1,0:T(8,128)(2,1)S(1)} %copy-done), kind=kLoop, calls=%fused_computation | loop fusion | flops 16384 | bytes 81920 | tf_op jit(solution)/shard_map/add | solution.py:431
Async XLA Ops:
  0.0 25.4 %copy-start = (bf16[2,64,64]{2,1,0:T(8,128)(2,1)S(1)}, bf16[2,64,64]{2,1,0:T(8,128)(2,1)}, u32[]{:S(2)}) copy-start(bf16[2,64,64]{2,1,0:T(8,128)(2,1)} %param.9) | copy-start | bytes 49156

commit v2 on v1

--- a/solution.py
+++ b/solution.py
@@ -79,9 +79,9 @@
 def quench_kernel(
     row_count, occupied, disorder, region_cols, cheb_coef, out,
     fields, turned, levels, hot, window, picks, operator, product, kept, leaving,
-    crossed, outgoing, incoming, columns, weights,
-    load_sem, level_send, level_recv, field_send, field_recv,
-    cross_send, cross_recv, block_send, block_recv,
+    nearby, crossed, outgoing, incoming, columns, weights,
+    here, load_sem, level_send, level_recv, field_send, field_recv,
+    near_send, near_recv, cross_send, cross_recv, block_send, block_recv,
 ):
     r = lax.axis_index("rows")
     o = lax.axis_index("orb")
@@ -101,6 +101,7 @@
     pair = r + 1 - 2 * place
     across = (r + half) % row_count
     owner = g == side
+    passer = jnp.logical_not(owner)
     spots = 2 * LANES
 
     def remote(src, dst, send, recv, row, orb):
@@ -116,11 +117,10 @@
             barrier, inc=1, device_id={"rows": row, "orb": orb}, device_id_type=MESH
         )
 
-    has_left, has_right = r > 0, r < row_count - 1
-    pl.when(has_left)(lambda: greet((r + row_count - 1) % row_count, o))
-    pl.when(has_right)(lambda: greet((r + 1) % row_count, o))
     for k in range(1, 4):
         greet(r, (o + k) % 4)
+    for k in range(1, row_count):
+        pl.when(r + k < row_count)(lambda k=k: greet((r + k) % row_count, o))
 
     def chunk(i, which):
         return occupied.at[:, i, :, pl.ds(pl.multiple_of(which * LANES, LANES), LANES)]
@@ -132,27 +132,34 @@
     ]
     for load in loads:
         load.start()
-    own_loads = [
-        pltpu.make_async_copy(chunk(i, place), fields.at[0, i], field_recv.at[0, i])
-        for i in range(band)
-    ]
-    for load in own_loads:
-        load.start()
+    def own_load(slot, i):
+        return pltpu.make_async_copy(
+            chunk(i, place if slot == 0 else 1 - place), fields.at[slot, i], field_recv.at[slot, i]
+        )
+
+    for i in range(band):
+        own_load(0, i).start()
+
+    @pl.when(owner)
+    def _():
+        for i in range(band):
+            own_load(1, i).start()
+
     for load in loads:
         load.wait()
 
-    pl.semaphore_wait(
-        barrier, 3 + jnp.where(has_left, 1, 0) + jnp.where(has_right, 1, 0)
-    )
-
-    def level_copy(first, count, way, kind, row):
-        part = levels.at[pl.ds(first, count)]
-        return remote(part, part, level_send.at[kind], level_recv.at[way], row, o)
-
-    to_left = functools.partial(level_copy, r, 1, 1, 0, (r + row_count - 1) % row_count)
-    to_right = functools.partial(level_copy, r, 1, 0, 1, (r + 1) % row_count)
-    pl.when(has_left)(lambda: to_left().start())
-    pl.when(has_right)(lambda: to_right().start())
+    pl.semaphore_wait(barrier, 3 + r)
+
+    def level_copy(slot, kind, row):
+        return remote(
+            levels.at[slot], levels.at[slot], level_send.at[kind], level_recv.at[slot], row, o
+        )
+
+    def down(k):
+        return level_copy(r, k - 1, (r + row_count - k) % row_count)
+
+    def up(k):
+        return level_copy(r, row_count + k - 2, (r + k) % row_count)
 
     def field_copy(i):
         return remote(
@@ -160,8 +167,27 @@
             field_recv.at[1, i], pair, o,
         )
 
-    for i in range(band):
-        field_copy(i).start()
+    def answer(k):
+        pl.semaphore_signal(
+            here.at[r], inc=1,
+            device_id={"rows": (r + row_count - k) % row_count, "orb": o}, device_id_type=MESH,
+        )
+
+    def send_fields():
+        for i in range(band):
+            field_copy(i).start()
+
+    def climb(k):
+        pl.semaphore_wait(here.at[(r + k) % row_count], 1)
+        up(k).start()
+
+    for k in range(1, row_count):
+        pl.when(r >= k)(functools.partial(answer, k))
+    for k in range(row_count - 1, 0, -1):
+        pl.when(r >= k)(lambda k=k: down(k).start())
+    pl.when(passer & (place == 1))(send_fields)
+    pl.when(r + 1 < row_count)(functools.partial(climb, 1))
+    pl.when(passer & (place == 0))(send_fields)
 
     lane = lax.broadcasted_iota(jnp.int32, (1, LANES), 1)
     cols = jnp.zeros((1, LANES), jnp.int32)
@@ -190,31 +216,20 @@
             )
 
     for i in range(band):
-        own_loads[i].wait()
+        own_load(0, i).wait()
         turn(0, i)
 
-    @pl.when(has_left)
+    @pl.when(owner)
     def _():
-        level_copy((r + row_count - 1) % row_count, 1, 0, 1, r).wait_recv()
-
-    @pl.when(has_right)
-    def _():
-        level_copy((r + 1) % row_count, 1, 1, 0, r).wait_recv()
-
-    middle = (r > 0) & (r < row_count - 1)
-    behind = (row_count - 1) * side
-    both_far = functools.partial(level_copy, half * side, half, 2, 2, (row_count - 1) * (1 - side))
-    one_near = functools.partial(level_copy, behind, 1, 2, 3, row_count - 1 - r)
-
-    @pl.when(middle)
-    def _():
-        both_far().start()
-        one_near().start()
-        level_copy((row_count - 1) * (1 - side), 1, 2, 3, r).wait_recv()
-
-    @pl.when(jnp.logical_not(middle))
-    def _():
-        level_copy(half * (1 - side), half, 2, 2, r).wait_recv()
+        for i in range(band):
+            own_load(1, i).wait()
+            turn(1, i)
+
+    for k in range(2, row_count):
+        pl.when(r + k < row_count)(functools.partial(climb, k))
+    for k in range(1, row_count):
+        slot = (r + k) % row_count
+        level_copy(slot, 0, (r + 1) % row_count).wait_recv()
 
     onsite = jnp.concatenate([levels[k] for k in range(row_count)], axis=0)
     onsite = (onsite.astype(jnp.float32) * LEVEL_STEP).astype(jnp.bfloat16)
@@ -282,56 +297,63 @@
                         part * spots : (part + 1) * spots,
                     ] = upper * picks[j] + lower * picks[(j - 1) % strips]
 
-    def applied(slot):
+    def applied(slot, at):
         rows = slice(slot * band * width, (slot + 1) * band * width)
-        return jnp.dot(
-            turned[:, rows], operator[0, rows, :], preferred_element_type=jnp.float32
-        ) + jnp.dot(turned[:, rows], operator[1, rows, :], preferred_element_type=jnp.float32)
+        ats = slice(at * band * width, (at + 1) * band * width)
+        total = jnp.dot(
+            turned[:, rows], operator[0, ats, :], preferred_element_type=jnp.float32
+        ) + jnp.dot(turned[:, rows], operator[1, ats, :], preferred_element_type=jnp.float32)
+        return total
+
+    def pieces(total):
+        return (
+            total[:LANES, :spots] - total[LANES:, spots:],
+            total[LANES:, :spots] + total[:LANES, spots:],
+        )
+
+    def near_copy():
+        return remote(leaving, nearby, near_send, near_recv, pair, o)
+
+    def cross_copy():
+        return remote(leaving, crossed, cross_send, cross_recv, across, o)
+
+    def block_copy(chip, part, slot):
+        return remote(
+            outgoing.at[2 * chip + part], incoming.at[slot], block_send.at[2 * chip + part],
+            block_recv.at[slot], chip // 2, 2 * (chip % 2) + part,
+        )
 
     for i in range(band):
         expand(0, i)
-    product[...] = applied(0)
-    for i in range(band):
-        expand(1, i)
-    for i in range(band):
-        remote(
-            fields.at[1, i], fields.at[1, i], field_send.at[i], field_recv.at[1, i], pair, o
-        ).wait_recv()
-        turn(1, i)
-    total = product[...] + applied(1)
-    sum0 = total[:LANES, :spots] - total[LANES:, spots:]
-    sum1 = total[LANES:, :spots] + total[:LANES, spots:]
-
-    def cross_copy():
-        return remote(leaving, crossed, cross_send, cross_recv, across, o)
-
-    def block_copy(k, part, slot):
-        to = (mine + k) % chips
-        place_of = 2 * to + part
-        return remote(
-            outgoing.at[place_of], incoming.at[slot], block_send.at[2 * k + part],
-            block_recv.at[slot], to // 2, 2 * (to % 2) + part,
-        )
-
-    def mate_copy():
-        return remote(
-            outgoing.at[2 * mine + 1 - g], incoming.at[mine], block_send.at[0],
-            block_recv.at[mine], r, 2 * x + 1 - g,
-        )
-
-    @pl.when(jnp.logical_not(owner))
+
+    @pl.when(passer)
     def _():
-        leaving[0] = sum0.astype(jnp.bfloat16)
-        leaving[1] = sum1.astype(jnp.bfloat16)
+        product[...] = applied(0, 0)
+        for i in range(band):
+            expand(1, i)
+        for i in range(band):
+            field_copy(i).wait_recv()
+            turn(1, i)
+        parts = pieces(product[...] + applied(1, 1))
+        leaving[0] = parts[0].astype(jnp.bfloat16)
+        leaving[1] = parts[1].astype(jnp.bfloat16)
         cross_copy().start()
 
     @pl.when(owner)
     def _():
-        kept[0] = sum0
-        kept[1] = sum1
+        parts = pieces(applied(1, 0))
+        leaving[0] = parts[0].astype(jnp.bfloat16)
+        leaving[1] = parts[1].astype(jnp.bfloat16)
+        near_copy().start()
+        parts = pieces(applied(0, 0))
+        kept[0] = parts[0]
+        kept[1] = parts[1]
+        near_copy().wait_recv()
         cross_copy().wait_recv()
         evolved = [
-            (kept[part] + crossed[part].astype(jnp.float32)).astype(jnp.bfloat16).T
+            (kept[part] + nearby[part].astype(jnp.float32) + crossed[part].astype(jnp.float32))
+            .astype(jnp.bfloat16)
+            .T
             for part in range(2)
         ]
         left = jnp.concatenate([evolved[0], evolved[1]], axis=1)
@@ -350,39 +372,43 @@
                 outgoing[4 * row + column] = blocks[
                     row * tile : (row + 1) * tile, column * LANES : (column + 1) * LANES
                 ]
-        for k in range(chips - 1, 0, -1):
+        for chip in range(chips):
             for part in range(2):
-                block_copy(k, part, mine).start()
-        mate_copy().start()
+
+                @pl.when((mine != chip) | (g != part))
+                def _():
+                    block_copy(chip, part, mine).start()
+
         incoming[mine] = outgoing[2 * mine + g]
 
-    pl.when(jnp.logical_not(owner))(lambda: mate_copy().wait_recv())
+    pl.when(passer)(lambda: block_copy(0, 0, mine).wait_recv())
     total = incoming[mine].astype(jnp.float32)
     for k in range(1, chips):
         slot = (mine + chips - k) % chips
-        block_copy(k, 0, slot).wait_recv()
+        block_copy(0, 0, slot).wait_recv()
         total = total + incoming[slot].astype(jnp.float32)
     out[0] = total[:, :tile]
     out[1] = total[:, tile:]
 
-    pl.when(has_left)(lambda: to_left().wait_send())
-    pl.when(has_right)(lambda: to_right().wait_send())
-
-    @pl.when(middle)
+    for k in range(1, row_count):
+        pl.when(r >= k)(lambda k=k: down(k).wait_send())
+        pl.when(r + k < row_count)(lambda k=k: up(k).wait_send())
+
+    @pl.when(passer)
     def _():
-        both_far().wait_send()
-        one_near().wait_send()
-
-    for i in range(band):
-        field_copy(i).wait_send()
-    pl.when(jnp.logical_not(owner))(lambda: cross_copy().wait_send())
+        for i in range(band):
+            field_copy(i).wait_send()
+        cross_copy().wait_send()
 
     @pl.when(owner)
     def _():
-        mate_copy().wait_send()
-        for k in range(1, chips):
+        near_copy().wait_send()
+        for chip in range(chips):
             for part in range(2):
-                block_copy(k, part, mine).wait_send()
+
+                @pl.when((mine != chip) | (g != part))
+                def _():
+                    block_copy(chip, part, mine).wait_send()
 
 
 def fused_step(row_count, occupied, disorder, region_cols, cheb_coef, prior_corr):
@@ -412,15 +438,19 @@
             pltpu.VMEM((2, LANES, spots), jnp.float32),
             pltpu.VMEM((2, LANES, spots), jnp.bfloat16),
             pltpu.VMEM((2, LANES, spots), jnp.bfloat16),
+            pltpu.VMEM((2, LANES, spots), jnp.bfloat16),
             pltpu.VMEM((2 * chips, tile, LANES), jnp.bfloat16),
             pltpu.VMEM((chips, tile, LANES), jnp.bfloat16),
             pltpu.SMEM(region_cols.shape, jnp.int32),
             pltpu.SMEM(cheb_coef.shape, jnp.float32),
+            pltpu.SemaphoreType.REGULAR((row_count,)),
             dma((3,)),
-            dma((4,)),
-            dma((3,)),
+            dma((2 * row_count - 2,)),
+            dma((row_count,)),
             dma((band,)),
             dma((2, band)),
+            dma,
+            dma,
             dma,
             dma,
             dma((2 * chips,)),

time: 26.2 us -> 21.4 us (0.82)
  Pallas kernels: 25.4 us -> 20.6 us
    pallas_call x1, Pallas kernels: 25.4 us -> 20.6 us  [fused_step(): pl.pallas_call(functools.partial(quench_kernel, row_count), out_shape=plt...]
where the time goes in v2:
time: 21.4 us; the launch traced here: 21.3 us
  Pallas kernels  20.6 us (96%)
  other arithmetic  0.64 us (3%)
    pallas_call x1, Pallas kernels, fused_step(): pl.pallas_call(functools.partial(quench_kernel, row_count), out_shape=plt...  20.6 us
    add x1, other arithmetic, fused_step(): return prior_corr.astype(jnp.float32) + corr  0.64 us

profile of v2, /device:TPU:0, one launch (start us, length us, event | category | flops | bytes accessed | tf_op | source)
XLA Modules:
  0.0 21.3 jit_solution(5257793227535815159)
XLA Ops:
  0.0 0.0 copy-start
  0.0 20.6 %shard_map.55 = f32[2,64,64]{2,1,0:T(8,128)S(1)} custom-call(bf16[2,2,256,256]{3,2,1,0:T(8,128)(2,1)} %occupied.1, s32[2,256]{1,0:T(2,128)} %disorder.1, s32[32]{0:T(128)} %region_cols.1, f32[2,8]{1,0:T(2,128)} %cheb_coef.1), custom_call_target="tpu_custom_call" | custom-call | tf_op jit(solution)/shard_map/pallas_call | solution.py:424
  20.6 0.0 copy-done
  20.6 0.6 %convert_add_fusion = f32[2,64,64]{2,1,0:T(8,128)} fusion(f32[2,64,64]{2,1,0:T(8,128)S(1)} %shard_map.55, bf16[2,64,64]{2,1,0:T(8,128)(2,1)S(1)} %copy-done), kind=kLoop, calls=%fused_computation | loop fusion | flops 16384 | bytes 81920 | tf_op jit(solution)/shard_map/add | solution.py:461
Async XLA Ops:
  0.0 20.6 %copy-start = (bf16[2,64,64]{2,1,0:T(8,128)(2,1)S(1)}, bf16[2,64,64]{2,1,0:T(8,128)(2,1)}, u32[]{:S(2)}) copy-start(bf16[2,64,64]{2,1,0:T(8,128)(2,1)} %param.9) | copy-start | bytes 49156

commit v3 on v2

--- a/solution.py
+++ b/solution.py
@@ -145,14 +145,11 @@
         for i in range(band):
             own_load(1, i).start()
 
-    for load in loads:
-        load.wait()
-
     pl.semaphore_wait(barrier, 3 + r)
 
     def level_copy(slot, kind, row):
         return remote(
-            levels.at[slot], levels.at[slot], level_send.at[kind], level_recv.at[slot], row, o
+            disorder, levels.at[slot], level_send.at[kind], level_recv.at[slot], row, o
         )
 
     def down(k):
@@ -188,6 +185,8 @@
     pl.when(passer & (place == 1))(send_fields)
     pl.when(r + 1 < row_count)(functools.partial(climb, 1))
     pl.when(passer & (place == 0))(send_fields)
+    for load in loads:
+        load.wait()
 
     lane = lax.broadcasted_iota(jnp.int32, (1, LANES), 1)
     cols = jnp.zeros((1, LANES), jnp.int32)
@@ -292,30 +291,41 @@
             for kind, value in ((0, high), (1, low)):
                 upper, lower = value[:FRAME], value[FRAME:]
                 for j in range(strips):
-                    operator[
-                        kind, k * width + j * FRAME : k * width + (j + 1) * FRAME,
-                        part * spots : (part + 1) * spots,
-                    ] = upper * picks[j] + lower * picks[(j - 1) % strips]
-
-    def applied(slot, at):
+                    strip = upper * picks[j] + lower * picks[(j - 1) % strips]
+                    rows = slice(k * width + j * FRAME, k * width + (j + 1) * FRAME)
+                    for s in range(2):
+                        operator[kind, s, rows, part * LANES : (part + 1) * LANES] = strip[
+                            :, s * LANES : (s + 1) * LANES
+                        ]
+
+    def applied(slot, at, s):
         rows = slice(slot * band * width, (slot + 1) * band * width)
         ats = slice(at * band * width, (at + 1) * band * width)
-        total = jnp.dot(
-            turned[:, rows], operator[0, ats, :], preferred_element_type=jnp.float32
-        ) + jnp.dot(turned[:, rows], operator[1, ats, :], preferred_element_type=jnp.float32)
-        return total
+        return jnp.dot(
+            turned[:, rows], operator[0, s, ats, :], preferred_element_type=jnp.float32
+        ) + jnp.dot(turned[:, rows], operator[1, s, ats, :], preferred_element_type=jnp.float32)
 
     def pieces(total):
         return (
-            total[:LANES, :spots] - total[LANES:, spots:],
-            total[LANES:, :spots] + total[:LANES, spots:],
-        )
-
-    def near_copy():
-        return remote(leaving, nearby, near_send, near_recv, pair, o)
-
-    def cross_copy():
-        return remote(leaving, crossed, cross_send, cross_recv, across, o)
+            total[:LANES, :LANES] - total[LANES:, LANES:],
+            total[LANES:, :LANES] + total[:LANES, LANES:],
+        )
+
+    def near_copy(s):
+        return remote(
+            leaving.at[s], nearby.at[s], near_send.at[s], near_recv.at[s], pair, o
+        )
+
+    def cross_copy(s):
+        return remote(
+            leaving.at[s], crossed.at[s], cross_send.at[s], cross_recv.at[s], across, o
+        )
+
+    def leave(s, total, copy):
+        parts = pieces(total)
+        for part in range(2):
+            leaving[s, part] = parts[part].astype(jnp.bfloat16)
+        copy(s).start()
 
     def block_copy(chip, part, slot):
         return remote(
@@ -328,52 +338,51 @@
 
     @pl.when(passer)
     def _():
-        product[...] = applied(0, 0)
+        for s in range(2):
+            product[s] = applied(0, 0, s)
         for i in range(band):
             expand(1, i)
         for i in range(band):
             field_copy(i).wait_recv()
             turn(1, i)
-        parts = pieces(product[...] + applied(1, 1))
-        leaving[0] = parts[0].astype(jnp.bfloat16)
-        leaving[1] = parts[1].astype(jnp.bfloat16)
-        cross_copy().start()
+        for s in range(2):
+            leave(s, product[s] + applied(1, 1, s), cross_copy)
 
     @pl.when(owner)
     def _():
-        parts = pieces(applied(1, 0))
-        leaving[0] = parts[0].astype(jnp.bfloat16)
-        leaving[1] = parts[1].astype(jnp.bfloat16)
-        near_copy().start()
-        parts = pieces(applied(0, 0))
-        kept[0] = parts[0]
-        kept[1] = parts[1]
-        near_copy().wait_recv()
-        cross_copy().wait_recv()
-        evolved = [
-            (kept[part] + nearby[part].astype(jnp.float32) + crossed[part].astype(jnp.float32))
-            .astype(jnp.bfloat16)
-            .T
-            for part in range(2)
-        ]
-        left = jnp.concatenate([evolved[0], evolved[1]], axis=1)
-        flipped = jnp.concatenate([-evolved[1], evolved[0]], axis=1)
+        for s in range(2):
+            parts = pieces(applied(0, 0, s))
+            kept[s, 0] = parts[0]
+            kept[s, 1] = parts[1]
+        for s in range(2):
+            leave(s, applied(1, 0, s), near_copy)
+        for s in range(2):
+            near_copy(s).wait_recv()
+            kept[s] = kept[s] + nearby[s].astype(jnp.float32)
+        lefts, turns = [], []
+        for s in range(2):
+            cross_copy(s).wait_recv()
+            whole = (kept[s] + crossed[s].astype(jnp.float32)).astype(jnp.bfloat16)
+            real_part, imag_part = whole[0].T, whole[1].T
+            lefts.append(jnp.concatenate([real_part, imag_part], axis=1))
+            turns.append(jnp.concatenate([-imag_part, real_part], axis=1))
+        left = jnp.concatenate(lefts, axis=0)
+        flipped = jnp.concatenate(turns, axis=0)
         rights = []
         for column in range(4):
             rows = slice(column * tile, (column + 1) * tile)
             rights.append(left[rows])
             rights.append(flipped[rows])
-        blocks = lax.dot_general(
-            left, jnp.concatenate(rights, axis=0), (((1,), (1,)), ((), ())),
-            preferred_element_type=jnp.float32,
-        ).astype(jnp.bfloat16)
-        for row in range(row_count):
+        right = jnp.concatenate(rights, axis=0)
+        for row in (0, *range(row_count - 1, 0, -1)):
+            blocks = lax.dot_general(
+                left[row * tile : (row + 1) * tile], right, (((1,), (1,)), ((), ())),
+                preferred_element_type=jnp.float32,
+            ).astype(jnp.bfloat16)
             for column in range(4):
-                outgoing[4 * row + column] = blocks[
-                    row * tile : (row + 1) * tile, column * LANES : (column + 1) * LANES
-                ]
-        for chip in range(chips):
-            for part in range(2):
+                outgoing[4 * row + column] = blocks[:, column * LANES : (column + 1) * LANES]
+            for column in range(4):
+                chip, part = 2 * row + column // 2, column % 2
 
                 @pl.when((mine != chip) | (g != part))
                 def _():
@@ -398,11 +407,13 @@
     def _():
         for i in range(band):
             field_copy(i).wait_send()
-        cross_copy().wait_send()
+        for s in range(2):
+            cross_copy(s).wait_send()
 
     @pl.when(owner)
     def _():
-        near_copy().wait_send()
+        for s in range(2):
+            near_copy(s).wait_send()
         for chip in range(chips):
             for part in range(2):
 
@@ -433,12 +444,12 @@
             pltpu.VMEM((2 * terms - 3, width, LANES), jnp.bfloat16),
             pltpu.VMEM((2, 2 * FRAME * height, LANES), jnp.float32),
             pltpu.VMEM((width // FRAME, FRAME, spots), jnp.bfloat16),
-            pltpu.VMEM((2, height // 2 * width, 2 * spots), jnp.bfloat16),
-            pltpu.VMEM((2 * LANES, 2 * spots), jnp.float32),
-            pltpu.VMEM((2, LANES, spots), jnp.float32),
-            pltpu.VMEM((2, LANES, spots), jnp.bfloat16),
-            pltpu.VMEM((2, LANES, spots), jnp.bfloat16),
-            pltpu.VMEM((2, LANES, spots), jnp.bfloat16),
+            pltpu.VMEM((2, 2, height // 2 * width, spots), jnp.bfloat16),
+            pltpu.VMEM((2, 2 * LANES, spots), jnp.float32),
+            pltpu.VMEM((2, 2, LANES, LANES), jnp.float32),
+            pltpu.VMEM((2, 2, LANES, LANES), jnp.bfloat16),
+            pltpu.VMEM((2, 2, LANES, LANES), jnp.bfloat16),
+            pltpu.VMEM((2, 2, LANES, LANES), jnp.bfloat16),
             pltpu.VMEM((2 * chips, tile, LANES), jnp.bfloat16),
             pltpu.VMEM((chips, tile, LANES), jnp.bfloat16),
             pltpu.SMEM(region_cols.shape, jnp.int32),
@@ -449,10 +460,10 @@
             dma((row_count,)),
             dma((band,)),
             dma((2, band)),
-            dma,
-            dma,
-            dma,
-            dma,
+            dma((2,)),
+            dma((2,)),
+            dma((2,)),
+            dma((2,)),
             dma((2 * chips,)),
             dma((chips,)),
         ],

time: 21.4 us -> 21.2 us (level)
  no operation moved by 1% of the time
where the time goes in v3:
time: 21.2 us; the launch traced here: 21.1 us
  Pallas kernels  20.4 us (96%)
  other arithmetic  0.64 us (3%)
    pallas_call x1, Pallas kernels, fused_step(): pl.pallas_call(functools.partial(quench_kernel, row_count), out_shape=plt...  20.4 us
    add x1, other arithmetic, fused_step(): return prior_corr.astype(jnp.float32) + corr  0.64 us

profile of v3, /device:TPU:0, one launch (start us, length us, event | category | flops | bytes accessed | tf_op | source)
XLA Modules:
  0.0 21.1 jit_solution(1715981713022877088)
XLA Ops:
  0.0 0.0 copy-start
  0.0 20.4 %shard_map.55 = f32[2,64,64]{2,1,0:T(8,128)S(1)} custom-call(bf16[2,2,256,256]{3,2,1,0:T(8,128)(2,1)} %occupied.1, s32[2,256]{1,0:T(2,128)} %disorder.1, s32[32]{0:T(128)} %region_cols.1, f32[2,8]{1,0:T(2,128)} %cheb_coef.1), custom_call_target="tpu_custom_call" | custom-call | tf_op jit(solution)/shard_map/pallas_call | solution.py:435
  20.4 0.0 copy-done
  20.4 0.6 %convert_add_fusion = f32[2,64,64]{2,1,0:T(8,128)} fusion(f32[2,64,64]{2,1,0:T(8,128)S(1)} %shard_map.55, bf16[2,64,64]{2,1,0:T(8,128)(2,1)S(1)} %copy-done), kind=kLoop, calls=%fused_computation | loop fusion | flops 16384 | bytes 81920 | tf_op jit(solution)/shard_map/add | solution.py:472
Async XLA Ops:
  0.0 20.4 %copy-start = (bf16[2,64,64]{2,1,0:T(8,128)(2,1)S(1)}, bf16[2,64,64]{2,1,0:T(8,128)(2,1)}, u32[]{:S(2)}) copy-start(bf16[2,64,64]{2,1,0:T(8,128)(2,1)} %param.9) | copy-start | bytes 49156

commit v4 on v3

--- a/solution.py
+++ b/solution.py
@@ -80,7 +80,7 @@
     row_count, occupied, disorder, region_cols, cheb_coef, out,
     fields, turned, levels, hot, window, picks, operator, product, kept, leaving,
     nearby, crossed, outgoing, incoming, columns, weights,
-    here, load_sem, level_send, level_recv, field_send, field_recv,
+    here, beside, complete, load_sem, level_send, level_recv, field_send, field_recv,
     near_send, near_recv, cross_send, cross_recv, block_send, block_recv,
 ):
     r = lax.axis_index("rows")
@@ -117,8 +117,9 @@
             barrier, inc=1, device_id={"rows": row, "orb": orb}, device_id_type=MESH
         )
 
-    for k in range(1, 4):
-        greet(r, (o + k) % 4)
+    greet(r, 2 * x + 1 - g)
+    for column in range(2, 4):
+        pl.when(x == 0)(lambda column=column: greet(r, column))
     for k in range(1, row_count):
         pl.when(r + k < row_count)(lambda k=k: greet((r + k) % row_count, o))
 
@@ -145,7 +146,7 @@
         for i in range(band):
             own_load(1, i).start()
 
-    pl.semaphore_wait(barrier, 3 + r)
+    pl.semaphore_wait(barrier, 1 + 2 * x + r)
 
     def level_copy(slot, kind, row):
         return remote(
@@ -180,6 +181,14 @@
 
     for k in range(1, row_count):
         pl.when(r >= k)(functools.partial(answer, k))
+
+    def reply(column):
+        pl.semaphore_signal(
+            beside.at[g], inc=1, device_id={"rows": r, "orb": column}, device_id_type=MESH
+        )
+
+    for column in range(2):
+        pl.when(x == 1)(functools.partial(reply, column))
     for k in range(row_count - 1, 0, -1):
         pl.when(r >= k)(lambda k=k: down(k).start())
     pl.when(passer & (place == 1))(send_fields)
@@ -224,11 +233,36 @@
             own_load(1, i).wait()
             turn(1, i)
 
-    for k in range(2, row_count):
-        pl.when(r + k < row_count)(functools.partial(climb, k))
+    last = row_count - 1
+
+    def both_copy():
+        rows = levels.at[pl.ds(0, 2)]
+        return remote(rows, rows, level_send.at[row_count], level_recv.at[0], last, o)
+
+    pl.when(r + 2 < last)(functools.partial(climb, 2))
+
+    @pl.when(r == 1)
+    def _():
+        level_copy(0, 0, last).wait_recv()
+        pl.semaphore_wait(here.at[last], 1)
+        both_copy().start()
+
+    pl.when(r == 0)(lambda: pl.semaphore_wait(here.at[last], 1))
+    for column in range(2):
+        pl.when(x == 0)(lambda column=column: pl.semaphore_wait(beside.at[column], 1))
     for k in range(1, row_count):
-        slot = (r + k) % row_count
-        level_copy(slot, 0, (r + 1) % row_count).wait_recv()
+        pl.semaphore_signal(
+            complete.at[r], inc=1,
+            device_id={"rows": (r + k) % row_count, "orb": o}, device_id_type=MESH,
+        )
+    for slot in range(row_count):
+        if slot < 2:
+            pl.when((r != slot) & (r != last) & ((slot != 0) | (r != 1)))(
+                lambda slot=slot: level_copy(slot, 0, last).wait_recv()
+            )
+        else:
+            pl.when(r != slot)(lambda slot=slot: level_copy(slot, 0, last).wait_recv())
+    pl.when(r == last)(lambda: both_copy().wait_recv())
 
     onsite = jnp.concatenate([levels[k] for k in range(row_count)], axis=0)
     onsite = (onsite.astype(jnp.float32) * LEVEL_STEP).astype(jnp.bfloat16)
@@ -333,6 +367,9 @@
             block_recv.at[slot], chip // 2, 2 * (chip % 2) + part,
         )
 
+    for k in range(1, row_count):
+        pl.semaphore_wait(complete.at[(r + k) % row_count], 1)
+
     for i in range(band):
         expand(0, i)
 
@@ -374,19 +411,21 @@
             rights.append(left[rows])
             rights.append(flipped[rows])
         right = jnp.concatenate(rights, axis=0)
-        for row in (0, *range(row_count - 1, 0, -1)):
-            blocks = lax.dot_general(
-                left[row * tile : (row + 1) * tile], right, (((1,), (1,)), ((), ())),
-                preferred_element_type=jnp.float32,
-            ).astype(jnp.bfloat16)
-            for column in range(4):
-                outgoing[4 * row + column] = blocks[:, column * LANES : (column + 1) * LANES]
-            for column in range(4):
-                chip, part = 2 * row + column // 2, column % 2
-
-                @pl.when((mine != chip) | (g != part))
-                def _():
-                    block_copy(chip, part, mine).start()
+        for turn_of in range(2):
+            for row in (0, *range(row_count - 1, 0, -1)):
+                blocks = lax.dot_general(
+                    left[row * tile : (row + 1) * tile],
+                    right[turn_of * 2 * LANES : (turn_of + 1) * 2 * LANES],
+                    (((1,), (1,)), ((), ())), preferred_element_type=jnp.float32,
+                ).astype(jnp.bfloat16)
+                chip = 2 * row + turn_of
+                for part in range(2):
+                    outgoing[2 * chip + part] = blocks[:, part * LANES : (part + 1) * LANES]
+                for part in range(2):
+
+                    @pl.when((mine != chip) | (g != part))
+                    def _():
+                        block_copy(chip, part, mine).start()
 
         incoming[mine] = outgoing[2 * mine + g]
 
@@ -401,7 +440,9 @@
 
     for k in range(1, row_count):
         pl.when(r >= k)(lambda k=k: down(k).wait_send())
-        pl.when(r + k < row_count)(lambda k=k: up(k).wait_send())
+        if k < 3:
+            pl.when(r + k < row_count - (k - 1))(lambda k=k: up(k).wait_send())
+    pl.when(r == 1)(lambda: both_copy().wait_send())
 
     @pl.when(passer)
     def _():
@@ -455,6 +496,8 @@
             pltpu.SMEM(region_cols.shape, jnp.int32),
             pltpu.SMEM(cheb_coef.shape, jnp.float32),
             pltpu.SemaphoreType.REGULAR((row_count,)),
+            pltpu.SemaphoreType.REGULAR((2,)),
+            pltpu.SemaphoreType.REGULAR((row_count,)),
             dma((3,)),
             dma((2 * row_count - 2,)),
             dma((row_count,)),

time: 21.2 us -> 21 us (level)
    pallas_call x1, Pallas kernels: 20.4 us -> 20.2 us  [fused_step(): pl.pallas_call(functools.partial(quench_kernel, row_count), out_shape=plt...]
where the time goes in v4:
time: 21 us; the launch traced here: 20.8 us
  Pallas kernels  20.2 us (96%)
  other arithmetic  0.64 us (3%)
    pallas_call x1, Pallas kernels, fused_step(): pl.pallas_call(functools.partial(quench_kernel, row_count), out_shape=plt...  20.2 us
    add x1, other arithmetic, fused_step(): return prior_corr.astype(jnp.float32) + corr  0.64 us

profile of v4, /device:TPU:0, one launch (start us, length us, event | category | flops | bytes accessed | tf_op | source)
XLA Modules:
  0.0 20.8 jit_solution(7811213160148487041)
XLA Ops:
  0.0 0.0 copy-start
  0.0 20.2 %shard_map.55 = f32[2,64,64]{2,1,0:T(8,128)S(1)} custom-call(bf16[2,2,256,256]{3,2,1,0:T(8,128)(2,1)} %occupied.1, s32[2,256]{1,0:T(2,128)} %disorder.1, s32[32]{0:T(128)} %region_cols.1, f32[2,8]{1,0:T(2,128)} %cheb_coef.1), custom_call_target="tpu_custom_call" | custom-call | tf_op jit(solution)/shard_map/pallas_call | solution.py:476
  20.2 0.0 copy-done
  20.2 0.6 %convert_add_fusion = f32[2,64,64]{2,1,0:T(8,128)} fusion(f32[2,64,64]{2,1,0:T(8,128)S(1)} %shard_map.55, bf16[2,64,64]{2,1,0:T(8,128)(2,1)S(1)} %copy-done), kind=kLoop, calls=%fused_computation | loop fusion | flops 16384 | bytes 81920 | tf_op jit(solution)/shard_map/add | solution.py:515
Async XLA Ops:
  0.0 20.2 %copy-start = (bf16[2,64,64]{2,1,0:T(8,128)(2,1)S(1)}, bf16[2,64,64]{2,1,0:T(8,128)(2,1)}, u32[]{:S(2)}) copy-start(bf16[2,64,64]{2,1,0:T(8,128)(2,1)} %param.9) | copy-start | bytes 49156
